TPU v7x, 32 devices: a whole 2x2x4 slice. The times are simulated.
32 devices in a mesh: sec: 4 (over z), tile: 4 (over y, core), role: 2 (over x).
Axes of the slice: x: 2, y: 2, z: 4, core: 2. Of those that a mesh axis runs over, the one named last changes fastest.
Arguments:
- pressure: float32 [32, 256, 8192], P(None, 'sec', ('tile', 'role')), may hold values from -6 to 6
- cell_weight: float32 [8192], P(('tile', 'role')), may hold values from 0.25 to 4
- live_cells: int32 [8], replicated, may hold values from 341 to 1024, as said below
- mode_order: int32 [128], replicated, may hold values from 0 to 127, each once
Outputs:
- gram: float32 [128, 32, 32], P('sec', ('tile', 'role'))
Inputs may be any that keep to these rules, and one draw needn't show every extreme that they name: `live_cells`: at least one tile half is full. `mode_order`: each wavenumber appears once.
All inputs are finite; a program needn't handle non-finite values.
Results may differ from a plain program's by a relative error of at most 0.0003.
Values sent between devices are 32-bit elements; how exact they have to be, the bound alone decides.
A program may use at most 128 MiB of HBM per device.

v0:
```python
import math

import jax
import jax.numpy as jnp
from jax import lax
from jax.sharding import PartitionSpec as P


def time_table(count):
    steps = jnp.arange(count, dtype=jnp.int32)
    half = count // 2
    freqs = jnp.arange(half, dtype=jnp.int32)
    hann = 0.5 - 0.5 * jnp.cos(2.0 * math.pi * steps.astype(jnp.float32) / count)
    phase = 2.0 * math.pi * (freqs[:, None] * steps[None, :] % count).astype(jnp.float32) / count
    factor = math.sqrt(8.0 / (3.0 * count))
    return jnp.concatenate(
        [factor * hann[None, :] * jnp.cos(phase), -factor * hann[None, :] * jnp.sin(phase)], axis=0
    )


def angle_table(mode_order, angles):
    index = jnp.arange(angles, dtype=jnp.int32)
    phase = (
        2.0 * math.pi * (mode_order[:, None] * index[None, :] % angles).astype(jnp.float32) / angles
    )
    cosine = jnp.cos(phase) / math.sqrt(angles)
    sine = jnp.sin(phase) / math.sqrt(angles)
    return jnp.stack(
        [jnp.stack([cosine, sine], axis=1), jnp.stack([-sine, cosine], axis=1)], axis=0
    )


def on_device(pressure, cell_weight, live_cells, mode_order):
    hi = lax.Precision.HIGHEST
    snaps = pressure.shape[0]
    half = snaps // 2
    n_sec = lax.axis_size("sec")
    n_grp = lax.axis_size("tile") * lax.axis_size("role")
    angles = pressure.shape[1] * n_sec
    group_cells = pressure.shape[2]
    cell_dev = group_cells // n_sec
    modes = mode_order.shape[0]
    total_cells = group_cells * n_grp
    htab = time_table(snaps)
    atab = angle_table(mode_order, angles)
    arrived = lax.all_to_all(pressure, "sec", split_axis=2, concat_axis=1, tiled=True)
    spectra = jnp.einsum("rt,tqc->rqc", htab, arrived, precision=hi)
    split = spectra.reshape(2, half, angles, cell_dev)
    modal = jnp.einsum("okiq,ifqc->kofc", atab, split, precision=hi).reshape(modes, snaps, cell_dev)
    group = lax.axis_index("tile") * lax.axis_size("role") + lax.axis_index("role")
    live = lax.dynamic_slice_in_dim(live_cells, group, 1, 0)[0]
    owned = lax.all_to_all(modal, "sec", split_axis=0, concat_axis=2, tiled=True)
    position = jnp.arange(group_cells, dtype=jnp.int32)
    weighted = jnp.where(position < live, cell_weight / total_cells, jnp.float32(0.0))
    local_gram = jnp.einsum("kac,kbc->kab", owned * weighted[None, None, :], owned, precision=hi)
    result = lax.psum_scatter(local_gram, ("tile", "role"), scatter_dimension=1, tiled=True)
    return result


def solution(mesh):
    in_specs = (P(None, "sec", ("tile", "role")), P(("tile", "role")), P(), P())
    out_specs = P("sec", ("tile", "role"), None)
    return jax.shard_map(
        on_device, mesh=mesh, in_specs=in_specs, out_specs=out_specs, check_vma=False
    )
```

profile of v0, /device:TPU:0, one launch (start us, length us, event | category | flops | bytes accessed | tf_op | source)
XLA Modules:
  0.0 473.6 jit_solution(6145706416273522948)
XLA Ops:
  6.5 16.2 %copy.12 = f32[32,64,1024]{1,0,2:T(8,128)} copy(f32[32,64,1024]{2,1,0:T(8,128)} %param.4) | data formatting | bytes 16777216 | tf_op args[0]
  22.7 14.4 %reshape.145 = f32[4,1,524288]{2,1,0:T(1,128)} reshape(f32[1024,32,64]{2,1,0:T(8,128)} %bitcast.38) | data formatting | bytes 16777216
  37.1 0.0 copy-start.1
  37.1 6.5 %all-to-all-start = ((f32[4,1,524288]{2,1,0:T(1,128)}), f32[4,1,524288]{2,1,0:T(1,128)}, u32[]{:S(2)}, u32[]{:S(2)}) async-start(f32[4,1,524288]{2,1,0:T(1,128)} %reshape.145), calls=%async_computation | async-start | bytes 16777216 | tf_op jit(solution)/shard_map/all_to_all | solution.py:46
  43.7 0.1 sine_multiply_fusion.1
  43.8 0.0 copy-done.1
  43.8 0.6 sine_multiply_fusion
  44.4 183.2 %all-to-all-done = f32[4,1,524288]{2,1,0:T(1,128)} async-done(((f32[4,1,524288]{2,1,0:T(1,128)}), f32[4,1,524288]{2,1,0:T(1,128)}, u32[]{:S(2)}, u32[]{:S(2)}) %all-to-all-start) | async-done | bytes 8388640 | tf_op jit(solution)/shard_map/all_to_all | solution.py:46
  227.7 0.5 broadcast.237
  228.2 28.4 %reduce = f32[4,524288]{1,0:T(4,128)} reduce(f32[4,1,524288]{2,1,0:T(1,128)} %all-to-all-done, f32[]{:T(128)} %broadcast.237), dimensions={1}, to_apply=%all_to_all.26.reduce_sub_computation | reduce | bytes 16777220 | tf_op jit(solution)/shard_map/all_to_all | solution.py:46
  256.6 16.8 %reshape.146 = f32[1024,32,64]{2,1,0:T(8,128)} reshape(f32[4,524288]{1,0:T(4,128)} %reduce) | data formatting | bytes 16777216
  273.3 13.2 %copy.24 = f32[32,64,4,256]{3,2,1,0:T(4,128)} copy(f32[32,64,4,256]{1,0,3,2:T(8,128)} %bitcast.37) | data formatting | bytes 16777216 | tf_op jit(solution)/shard_map/all_to_all | solution.py:46
  286.5 8.2 %copy.25 = f32[32,4,64,256]{3,0,2,1:T(8,128)S(1)} copy(f32[32,4,64,256]{3,1,2,0:T(4,128)} %bitcast.40) | data formatting | bytes 16777216 | tf_op jit(solution)/shard_map/all_to_all | solution.py:46
  294.8 8.4 %convolution_bitcast_fusion = f32[2,16,256,256,1]{3,1,2,0,4:T(8,128)S(1)} fusion(f32[2,16,32,1]{2,1,3,0:T(8,128)S(1)} %bitcast.43, f32[32,256,256,1]{2,0,1,3:T(8,128)S(1)} %bitcast.41), kind=kOutput, calls=%fused_computation.4 | convolution fusion | flops 805306368 | bytes 16781312 | tf_op jit(solution)/shard_map/rt,tqc->rqc/dot_general | solution.py:47
  303.2 17.4 %fusion.4 = f32[128,2,16,256]{0,3,1,2:T(8,128)} fusion(f32[2,16,256,256,1]{3,1,2,0,4:T(8,128)S(1)} %convolution_bitcast_fusion, f32[1,128,2,256]{3,1,2,0:T(8,128)S(1)} %get-tuple-element.6, f32[1,128,2,256]{3,1,2,0:T(8,128)S(1)} %get-tuple-element.5), kind=kOutput, calls=%fused_computation.5 | convolution fusion | flops 6442582016 | bytes 13107200 | tf_op jit(solution)/shard_map/okiq,ifqc->kofc/dot_general | solution.py:49
  320.7 0.0 copy-start.2
  320.7 0.0 copy-start
  320.7 5.5 %copy.17 = f32[128,2,16,256]{3,2,1,0:T(8,128)} copy(f32[128,2,16,256]{0,3,1,2:T(8,128)} %fusion.4) | data formatting | bytes 8388608 | tf_op jit(solution)/shard_map/okiq,ifqc->kofc/transpose | solution.py:49
  326.2 4.8 %all-to-all-start.1 = ((f32[128,32,256]{2,1,0:T(8,128)}), f32[128,32,256]{2,1,0:T(8,128)}, u32[]{:S(2)}, u32[]{:S(2)}) async-start(f32[128,32,256]{2,1,0:T(8,128)} %bitcast.42), calls=%async_computation.1 | async-start | bytes 8388608 | tf_op jit(solution)/shard_map/all_to_all | solution.py:52
  331.1 0.5 reduce-scatter.2.cloned.1.call-start
  331.6 0.0 copy-done.2
  331.6 0.6 dynamic_slice.3
  332.2 0.0 copy-done
  332.2 0.6 multiply_select_fusion
  332.8 91.1 %all-to-all-done.1 = f32[128,32,256]{2,1,0:T(8,128)} async-done(((f32[128,32,256]{2,1,0:T(8,128)}), f32[128,32,256]{2,1,0:T(8,128)}, u32[]{:S(2)}, u32[]{:S(2)}) %all-to-all-start.1) | async-done | bytes 4194336 | tf_op jit(solution)/shard_map/all_to_all | solution.py:52
  424.0 2.7 copy.28
  426.7 4.1 fusion.2
  430.7 1.1 copy.19
  431.8 0.0 reduce-scatter.2.cloned.1.call-update
  431.9 33.2 %reduce-scatter.2.cloned.1.call-done = f32[32,4,32]{2,0,1:T(8,128)} async-done(((f32[32,32,32]{2,0,1:T(8,128)}), f32[32,4,32]{2,0,1:T(8,128)}) %reduce-scatter.2.cloned.1.call-update) | async-done | bytes 16400 | tf_op jit(solution)/shard_map/reduce_scatter | solution.py:56
  465.1 1.5 copy.20
  (4 shorter events, 0.1 us)
Async XLA Ops:
  37.1 6.7 %copy-start.1 = (s32[128]{0:T(128)S(1)}, s32[128]{0:T(128)}, u32[]{:S(2)}) copy-start(s32[128]{0:T(128)} %param.7) | copy-start | bytes 1540
  37.1 190.6 %all-to-all-start = ((f32[4,1,524288]{2,1,0:T(1,128)}), f32[4,1,524288]{2,1,0:T(1,128)}, u32[]{:S(2)}, u32[]{:S(2)}) async-start(f32[4,1,524288]{2,1,0:T(1,128)} %reshape.145), calls=%async_computation | async-start | bytes 16777216 | tf_op jit(solution)/shard_map/all_to_all | solution.py:46
  320.7 10.9 %copy-start.2 = (s32[8]{0:T(128)S(1)}, s32[8]{0:T(128)}, u32[]{:S(2)}) copy-start(s32[8]{0:T(128)} %param.6) | copy-start | bytes 100
  320.7 11.5 %copy-start = (f32[1024]{0:T(1024)S(1)}, f32[1024]{0:T(1024)}, u32[]{:S(2)}) copy-start(f32[1024]{0:T(1024)} %param.5) | copy-start | bytes 12292
  326.2 97.7 %all-to-all-start.1 = ((f32[128,32,256]{2,1,0:T(8,128)}), f32[128,32,256]{2,1,0:T(8,128)}, u32[]{:S(2)}, u32[]{:S(2)}) async-start(f32[128,32,256]{2,1,0:T(8,128)} %bitcast.42), calls=%async_computation.1 | async-start | bytes 8388608 | tf_op jit(solution)/shard_map/all_to_all | solution.py:52
  331.1 134.0 %reduce-scatter.2.cloned.1.call-start = ((), (), s32[]{:S(2)}) async-start(), calls=%async_computation.3 | async-start | bytes 589824 | tf_op jit(solution)/shard_map/reduce_scatter | solution.py:56
Sparse Core Ops, SparseCore 0:
  432.0 33.0 reduce-scatter.1
where the time goes:
time: 480 us; the launch traced here: 474 us
  waiting for transfers between devices  308 us (64%)
  local copies, waits for them, and re-layouts  80.7 us (17%)
  other arithmetic  29.9 us (6%)
  matrix products  29.9 us (6%)
  between operations  13.6 us (3%)
  starting transfers between devices  11.8 us (2%)
    all_to_all x1, waiting for transfers between devices, on_device(): lax.all_to_all(pressure, 'sec', split_axis=2, concat_axis=1, tiled=True)  183 us
    all_to_all x1, waiting for transfers between devices, on_device(): lax.all_to_all(modal, 'sec', split_axis=0, concat_axis=2, tiled=True)  91.1 us
    unnamed x9, local copies, waits for them, and re-layouts  47.3 us
    reduce_scatter x1, waiting for transfers between devices, on_device(): lax.psum_scatter(local_gram, ('tile', 'role'), scatter_dimension=1, tiled...  33.2 us
    all_to_all x1, other arithmetic, on_device(): lax.all_to_all(pressure, 'sec', split_axis=2, concat_axis=1, tiled=True)  28.4 us
    all_to_all x3, local copies, waits for them, and re-layouts, on_device(): lax.all_to_all(pressure, 'sec', split_axis=2, concat_axis=1, tiled=True)  21.9 us
    dot_general x1, matrix products, on_device(): jnp.einsum('okiq,ifqc->kofc', atab, split, precision=hi)  17.4 us
  transfers between devices with their start and end apart: 3, of which 3 were waited for; matrix products, arithmetic and copies ran while one was open for 0% of the time, Pallas kernels for 0%

commit v1 on v0

v1 whole, which is shorter than its diff:
```python
import functools
import math

import jax
import jax.numpy as jnp
from jax import lax
from jax.experimental import pallas as pl
from jax.experimental.pallas import tpu as pltpu
from jax.sharding import PartitionSpec as P

MESH = pl.DeviceIdType.MESH
LANES = 128
SUB = 8
F32 = jnp.float32
BF16 = jnp.bfloat16


def halves(x):
    hi = x.astype(BF16)
    lo = (x - hi.astype(F32)).astype(BF16)
    return hi, lo


def left_terms(x):
    hi, lo = halves(x)
    return jnp.concatenate([hi, hi, lo], axis=1)


def right_terms(x):
    hi, lo = halves(x)
    return jnp.concatenate([hi, lo, hi], axis=0)


def dot(a, b, dims=(((1,), (0,)), ((), ()))):
    return lax.dot_general(a, b, dims, preferred_element_type=F32)


def by_distance(i, me, n):
    right = n - 1 - me
    both = jnp.minimum(me, right)
    paired = i <= 2 * both
    delta = jnp.where(paired, (i + 1) // 2, i - both)
    up = jnp.where(paired, i % 2 == 1, me < right)
    return jnp.where(up, me + delta, me - delta)


def iota(shape, axis):
    return lax.broadcasted_iota(jnp.int32, shape, axis)


def time_terms(snaps):
    size = snaps * SUB
    row, col = iota((size, size), 0), iota((size, size), 1)
    half = snaps // 2
    r, t = row // SUB, col // SUB
    f = r % half
    hann = 0.5 - 0.5 * jnp.cos((2.0 * math.pi / snaps) * t.astype(F32))
    phase = (2.0 * math.pi / snaps) * ((f * t) % snaps).astype(F32)
    wave = jnp.where(r < half, jnp.cos(phase), -jnp.sin(phase))
    value = math.sqrt(8.0 / (3.0 * snaps)) * hann * wave
    return jnp.where(row % SUB == col % SUB, value, 0.0)


def angle_terms(modes_row, angles):
    modes = modes_row.shape[1]
    index = iota((angles, modes), 0)
    phase = (2.0 * math.pi / angles) * ((modes_row * index) % angles).astype(F32)
    scale = 1.0 / math.sqrt(angles)
    return jnp.concatenate([(jnp.cos(phase) * scale).T, (jnp.sin(phase) * scale).T], axis=0)


def kernel(n_sec, n_tile, n_role, p_ref, w_ref, live_ref, mode_ref, out_ref,
           recv, spec, zbuf, acc, reda, sb, redb, ttab, atab,
           send_sem, recv_sem, own_sem, sa_sem, ra_sem, sb_sem, rb_sem):
    me = lax.axis_index("sec")
    tile, role = lax.axis_index("tile"), lax.axis_index("role")
    n_grp = n_tile * n_role
    grp = tile * n_role + role
    snaps, q_loc, cells = p_ref.shape
    half = snaps // 2
    angles = q_loc * n_sec
    modes = mode_ref.shape[1]
    cell_dev = cells // n_sec
    subs = cell_dev // LANES
    pack = LANES // snaps
    part = snaps // n_grp

    def peer(o):
        other = lax.rem(grp + o, n_grp)
        return other, {"tile": other // n_role, "role": other % n_role}

    barrier = pltpu.get_barrier_semaphore()
    for o in range(1, n_sec):
        pl.semaphore_signal(barrier, inc=1, device_id={"sec": lax.rem(me + o, n_sec)}, device_id_type=MESH)
    for o in range(1, n_grp):
        pl.semaphore_signal(barrier, inc=1, device_id=peer(o)[1], device_id_type=MESH)
    pl.semaphore_wait(barrier, n_sec + n_grp - 2)

    def piece(owner, j):
        start = pl.multiple_of(owner * cell_dev + j * LANES, LANES)
        return p_ref.at[:, :, pl.ds(start, LANES)]

    def outgoing(i, j):
        dest = by_distance(i, me, n_sec)
        return pltpu.make_async_remote_copy(
            src_ref=piece(dest, j), dst_ref=recv.at[j, me],
            send_sem=send_sem.at[j, dest], recv_sem=recv_sem.at[j, me],
            device_id={"sec": dest}, device_id_type=MESH)

    def own(j):
        return pltpu.make_async_copy(piece(me, j), recv.at[j, me], own_sem.at[j])

    for j in range(subs):
        @pl.loop(1, n_sec)
        def _(i):
            outgoing(i, j).start()
    for j in range(subs):
        own(j).start()

    ttab[...] = left_terms(time_terms(snaps))
    atab[...] = left_terms(angle_terms(mode_ref[...], angles))
    live = live_ref[grp]
    total = float(cells * n_grp)
    wide = 2 if q_loc % (2 * SUB) == 0 else 1

    def to_spectra(j, src):
        for g in range(0, q_loc, wide * SUB):
            x = jnp.concatenate(
                [recv[j, src, :, g + u * SUB:g + (u + 1) * SUB, :].reshape(snaps * SUB, LANES) for u in range(wide)],
                axis=1)
            y = dot(ttab[...], right_terms(x))
            for u in range(wide):
                at = pl.multiple_of(src * q_loc + g + u * SUB, SUB)
                spec[:, pl.ds(at, SUB), :] = y[:, u * LANES:(u + 1) * LANES].reshape(snaps, SUB, LANES)

    for j in range(subs):
        own(j).wait()
        to_spectra(j, me)

        @pl.loop(1, n_sec)
        def _(i):
            src = by_distance(i, me, n_sec)
            pltpu.make_async_remote_copy(
                src_ref=recv.at[j, src], dst_ref=recv.at[j, src],
                send_sem=send_sem.at[j, src], recv_sem=recv_sem.at[j, src],
                device_id={"sec": src}, device_id_type=MESH).wait_recv()
            to_spectra(j, src)

        @pl.loop(0, half)
        def _(f):
            x = jnp.concatenate([spec[f], spec[half + f]], axis=1)
            y = dot(atab[...], right_terms(x))
            zbuf[pl.ds(f, modes, stride=snaps), :] = y[:modes, :LANES] + y[modes:, LANES:]
            zbuf[pl.ds(half + f, modes, stride=snaps), :] = y[:modes, LANES:] - y[modes:, :LANES]

        first = pl.multiple_of(me * cell_dev + j * LANES, LANES)
        position = first + iota((1, LANES), 1)
        weight = jnp.where(position < live, w_ref[:, pl.ds(first, LANES)] / total, 0.0)
        block = iota((snaps, LANES), 1) // snaps
        steps = SUB // part

        @pl.loop(0, modes // pack // steps)
        def _(h):
            rows = []
            for u in range(steps):
                at = pl.multiple_of((h * steps + u) * LANES, LANES)
                z = zbuf[pl.ds(at, LANES), :]
                zh, zl = halves(z)
                g4 = dot(left_terms(z * weight), jnp.concatenate([zh, zl, zh], axis=1), (((1,), (1,)), ((), ())))
                r = g4[:snaps]
                for b in range(1, pack):
                    r = jnp.where(block == b, g4[b * snaps:(b + 1) * snaps], r)
                rows.append(r)
            at = pl.multiple_of(h * SUB, SUB)
            for g in range(n_grp):
                new = jnp.concatenate([r[g * part:(g + 1) * part] for r in rows], axis=0)
                if j == 0:
                    acc[g, pl.ds(at, SUB), :] = new
                else:
                    acc[g, pl.ds(at, SUB), :] += new

    def share(o):
        other, device = peer(o)
        return pltpu.make_async_remote_copy(
            src_ref=acc.at[other], dst_ref=reda.at[grp],
            send_sem=sa_sem.at[other], recv_sem=ra_sem.at[grp],
            device_id=device, device_id_type=MESH)

    def shared(o):
        other, device = peer(o)
        return pltpu.make_async_remote_copy(
            src_ref=acc.at[other], dst_ref=reda.at[other],
            send_sem=sa_sem.at[other], recv_sem=ra_sem.at[other],
            device_id=device, device_id_type=MESH)

    for o in range(1, n_grp):
        share(o).start()
    for o in range(1, n_grp):
        shared(o).wait_recv()
    rows = sb.shape[1]
    for s in range(n_sec):
        value = acc[grp, s * rows:(s + 1) * rows, :]
        for o in range(1, n_grp):
            value += reda[peer(o)[0], s * rows:(s + 1) * rows, :]
        sb[s] = value

    def last(s, slot):
        return pltpu.make_async_remote_copy(
            src_ref=sb.at[s], dst_ref=redb.at[slot],
            send_sem=sb_sem.at[s], recv_sem=rb_sem.at[slot],
            device_id={"sec": s}, device_id_type=MESH)

    for o in range(1, n_sec):
        last(lax.rem(me + o, n_sec), me).start()
    value = sb[me]
    for o in range(1, n_sec):
        s = lax.rem(me + o, n_sec)
        last(s, s).wait_recv()
        value += redb[s]
    out_ref[...] = value

    for j in range(subs):
        @pl.loop(1, n_sec)
        def _(i):
            outgoing(i, j).wait_send()
    for o in range(1, n_grp):
        share(o).wait_send()
    for o in range(1, n_sec):
        last(lax.rem(me + o, n_sec), me).wait_send()


def on_device(pressure, cell_weight, live_cells, mode_order):
    n_sec, n_tile, n_role = (lax.axis_size(a) for a in ("sec", "tile", "role"))
    n_grp = n_tile * n_role
    snaps, q_loc, cells = pressure.shape
    modes = mode_order.shape[0]
    angles = q_loc * n_sec
    subs = cells // n_sec // LANES
    pack = LANES // snaps
    part = snaps // n_grp
    rows = modes // pack * part
    own_rows = rows // n_sec
    vmem = pl.BlockSpec(memory_space=pltpu.VMEM)
    dma = pltpu.SemaphoreType.DMA
    packed = pl.pallas_call(
        functools.partial(kernel, n_sec, n_tile, n_role),
        out_shape=jax.ShapeDtypeStruct((own_rows, LANES), F32),
        in_specs=[pl.BlockSpec(memory_space=pl.ANY), vmem, pl.BlockSpec(memory_space=pltpu.SMEM), vmem],
        out_specs=vmem,
        scratch_shapes=[
            pltpu.VMEM((subs, n_sec, snaps, q_loc, LANES), F32),
            pltpu.VMEM((snaps, angles, LANES), F32),
            pltpu.VMEM((modes * snaps, LANES), F32),
            pltpu.VMEM((n_grp, rows, LANES), F32),
            pltpu.VMEM((n_grp, rows, LANES), F32),
            pltpu.VMEM((n_sec, own_rows, LANES), F32),
            pltpu.VMEM((n_sec, own_rows, LANES), F32),
            pltpu.VMEM((snaps * SUB, 3 * snaps * SUB), BF16),
            pltpu.VMEM((2 * modes, 3 * angles), BF16),
            dma((subs, n_sec)), dma((subs, n_sec)), dma((subs,)),
            dma((n_grp,)), dma((n_grp,)), dma((n_sec,)), dma((n_sec,)),
        ],
        compiler_params=pltpu.CompilerParams(
            collective_id=0, has_side_effects=True, vmem_limit_bytes=60 * 2**20),
        name="spod",
    )(pressure, cell_weight.reshape(1, cells), live_cells, mode_order.reshape(1, modes))
    out = packed.reshape(modes // pack // n_sec, part, pack, snaps)
    return out.transpose(0, 2, 1, 3).reshape(modes // n_sec, part, snaps)


def solution(mesh):
    in_specs = (P(None, "sec", ("tile", "role")), P(("tile", "role")), P(), P())
    out_specs = P("sec", ("tile", "role"), None)
    return jax.shard_map(
        on_device, mesh=mesh, in_specs=in_specs, out_specs=out_specs, check_vma=False
    )
```

time: 480 us -> 211 us (0.44); the launches traced: 474 us -> 211 us
  waiting for transfers between devices: 308 us -> 0 us
  Pallas kernels: 0 us -> 209 us
  local copies, waits for them, and re-layouts: 80.7 us -> 1.45 us
  matrix products: 29.9 us -> 0 us
  other arithmetic: 29.9 us -> 0 us
  between operations: 13.6 us -> 0.02 us
  starting transfers between devices: 11.8 us -> 0 us
    all_to_all x2 -> x0, waiting for transfers between devices: 274 us -> none  [the longest x1 183 us: on_device(): lax.all_to_all(pressure, 'sec', split_axis=2, concat_axis=1, tiled=True)]
    pallas_call x0 -> x1, Pallas kernels: none -> 209 us  [on_device(): pl.pallas_call(functools.partial(kernel, n_sec, n_tile, n_role), out_shap...]
    unnamed x9 -> x0, local copies, waits for them, and re-layouts: 47.3 us -> none
    reduce_scatter x1 -> x0, waiting for transfers between devices: 33.2 us -> none  [on_device(): lax.psum_scatter(local_gram, ('tile', 'role'), scatter_dimension=1, tiled...]
    dot_general x3 -> x0, matrix products: 29.9 us -> none  [the longest x1 17.4 us: on_device(): jnp.einsum('okiq,ifqc->kofc', atab, split, precision=hi)]
    all_to_all x1 -> x0, other arithmetic: 28.4 us -> none  [on_device(): lax.all_to_all(pressure, 'sec', split_axis=2, concat_axis=1, tiled=True)]
    all_to_all x4 -> x0, local copies, waits for them, and re-layouts: 24.6 us -> none  [the longest x3 21.9 us: on_device(): lax.all_to_all(pressure, 'sec', split_axis=2, concat_axis=1, tiled=True)]
    all_to_all x2 -> x0, starting transfers between devices: 11.3 us -> none  [the longest x1 6.48 us: on_device(): lax.all_to_all(pressure, 'sec', split_axis=2, concat_axis=1, tiled=True)]
  transfers between devices with their start and end apart: 3 -> 0, of which waited for: 3 -> 0; matrix products, arithmetic and copies ran while one was open for 0% -> 0% of each run, Pallas kernels for 0% -> 0%
where the time goes in v1:
time: 211 us
  Pallas kernels  209 us (99%)
    pallas_call x1, Pallas kernels, on_device(): pl.pallas_call(functools.partial(kernel, n_sec, n_tile, n_role), out_shap...  209 us

profile of v1, /device:TPU:0, one launch (start us, length us, event | category | flops | bytes accessed | tf_op | source)
XLA Modules:
  0.0 210.7 jit_solution(5666460223674371827)
XLA Ops:
  0.0 209.3 %spod.1 = f32[32,128]{1,0:T(8,128)} custom-call(f32[32,64,1024]{2,1,0:T(8,128)} %p_ref.1, f32[1,1024]{1,0:T(1,128)} %bitcast.5, s32[8]{0:T(128)} %live_ref.1, s32[1,128]{1,0:T(1,128)} %bitcast.6), custom_call_target="tpu_custom_call" | custom-call | tf_op jit(solution)/shard_map/spod/pallas_call | solution.py:245
  209.3 0.8 reshape.14
  210.1 0.6 copy.5

commit v2 on v1

--- a/solution.py
+++ b/solution.py
@@ -10,6 +10,8 @@
 
 MESH = pl.DeviceIdType.MESH
 LANES = 128
+UNROLL = 4
+STAGES = 4
 SUB = 8
 F32 = jnp.float32
 BF16 = jnp.bfloat16
@@ -35,13 +37,13 @@
     return lax.dot_general(a, b, dims, preferred_element_type=F32)
 
 
-def by_distance(i, me, n):
-    right = n - 1 - me
-    both = jnp.minimum(me, right)
-    paired = i <= 2 * both
-    delta = jnp.where(paired, (i + 1) // 2, i - both)
-    up = jnp.where(paired, i % 2 == 1, me < right)
-    return jnp.where(up, me + delta, me - delta)
+def partner(i, me, n):
+    x = jnp.where(i == 1, n - 1, i - 1)
+    other, bit = 0, 1
+    while bit < n:
+        other += (me // bit + x // bit) % 2 * bit
+        bit *= 2
+    return other
 
 
 def iota(shape, axis):
@@ -61,16 +63,15 @@
     return jnp.where(row % SUB == col % SUB, value, 0.0)
 
 
-def angle_terms(modes_row, angles):
-    modes = modes_row.shape[1]
-    index = iota((angles, modes), 0)
+def angle_terms(modes_row, angles, first, count):
+    index = first + iota((count, modes_row.shape[1]), 0)
     phase = (2.0 * math.pi / angles) * ((modes_row * index) % angles).astype(F32)
     scale = 1.0 / math.sqrt(angles)
     return jnp.concatenate([(jnp.cos(phase) * scale).T, (jnp.sin(phase) * scale).T], axis=0)
 
 
 def kernel(n_sec, n_tile, n_role, p_ref, w_ref, live_ref, mode_ref, out_ref,
-           recv, spec, zbuf, acc, reda, sb, redb, ttab, atab,
+           recv, spec, zbuf, acc, reda, sb, redb, ttab, atab, ltab, ypart,
            send_sem, recv_sem, own_sem, sa_sem, ra_sem, sb_sem, rb_sem):
     me = lax.axis_index("sec")
     tile, role = lax.axis_index("tile"), lax.axis_index("role")
@@ -84,6 +85,7 @@
     subs = cell_dev // LANES
     pack = LANES // snaps
     part = snaps // n_grp
+    split = q_loc % 16 == 0
 
     def peer(o):
         other = lax.rem(grp + o, n_grp)
@@ -101,7 +103,7 @@
         return p_ref.at[:, :, pl.ds(start, LANES)]
 
     def outgoing(i, j):
-        dest = by_distance(i, me, n_sec)
+        dest = partner(i, me, n_sec)
         return pltpu.make_async_remote_copy(
             src_ref=piece(dest, j), dst_ref=recv.at[j, me],
             send_sem=send_sem.at[j, dest], recv_sem=recv_sem.at[j, me],
@@ -118,7 +120,11 @@
         own(j).start()
 
     ttab[...] = left_terms(time_terms(snaps))
-    atab[...] = left_terms(angle_terms(mode_ref[...], angles))
+    atab[...] = left_terms(angle_terms(mode_ref[...], angles, 0, angles))
+    late = partner(n_sec - 1, me, n_sec)
+    late_at = pl.multiple_of(late * q_loc, SUB)
+    if split:
+        ltab[...] = left_terms(angle_terms(mode_ref[...], angles, late_at, q_loc))
     live = live_ref[grp]
     total = float(cells * n_grp)
     wide = 2 if q_loc % (2 * SUB) == 0 else 1
@@ -133,34 +139,67 @@
                 at = pl.multiple_of(src * q_loc + g + u * SUB, SUB)
                 spec[:, pl.ds(at, SUB), :] = y[:, u * LANES:(u + 1) * LANES].reshape(snaps, SUB, LANES)
 
+    stage_rows = acc.shape[1] // STAGES
+
+    def share(o, t, arriving=False):
+        other, device = peer(o)
+        at = pl.ds(t * stage_rows, stage_rows)
+        slot = other if arriving else grp
+        return pltpu.make_async_remote_copy(
+            src_ref=acc.at[other, at, :], dst_ref=reda.at[slot, at, :],
+            send_sem=sa_sem.at[t, other], recv_sem=ra_sem.at[t, slot],
+            device_id=device, device_id_type=MESH)
+
+    def arrive(i, j):
+        src = partner(i, me, n_sec)
+        pltpu.make_async_remote_copy(
+            src_ref=recv.at[j, src], dst_ref=recv.at[j, src],
+            send_sem=send_sem.at[j, src], recv_sem=recv_sem.at[j, src],
+            device_id={"sec": src}, device_id_type=MESH).wait_recv()
+        to_spectra(j, src)
+
+    def to_modal(f, y):
+        zbuf[pl.ds(f, modes, stride=snaps), :] = y[:modes, :LANES] + y[modes:, LANES:]
+        zbuf[pl.ds(half + f, modes, stride=snaps), :] = y[:modes, LANES:] - y[modes:, :LANES]
+
+    def products(f):
+        x = jnp.concatenate([spec[f], spec[half + f]], axis=1)
+        return dot(atab[...], right_terms(x))
+
     for j in range(subs):
         own(j).wait()
         to_spectra(j, me)
-
-        @pl.loop(1, n_sec)
+        early = split and j == subs - 1
+
+        @pl.loop(1, n_sec - 1 if early else n_sec)
         def _(i):
-            src = by_distance(i, me, n_sec)
-            pltpu.make_async_remote_copy(
-                src_ref=recv.at[j, src], dst_ref=recv.at[j, src],
-                send_sem=send_sem.at[j, src], recv_sem=recv_sem.at[j, src],
-                device_id={"sec": src}, device_id_type=MESH).wait_recv()
-            to_spectra(j, src)
-
-        @pl.loop(0, half)
-        def _(f):
-            x = jnp.concatenate([spec[f], spec[half + f]], axis=1)
-            y = dot(atab[...], right_terms(x))
-            zbuf[pl.ds(f, modes, stride=snaps), :] = y[:modes, :LANES] + y[modes:, LANES:]
-            zbuf[pl.ds(half + f, modes, stride=snaps), :] = y[:modes, LANES:] - y[modes:, :LANES]
+            arrive(i, j)
+
+        if early:
+            spec[:, pl.ds(late_at, q_loc), :] = jnp.zeros((snaps, q_loc, LANES), F32)
+
+            @pl.loop(0, half)
+            def _(f):
+                ypart[f] = products(f)
+
+            arrive(n_sec - 1, j)
+
+            @pl.loop(0, half, unroll=UNROLL)
+            def _(f):
+                x = jnp.concatenate([spec[f, pl.ds(late_at, q_loc), :], spec[half + f, pl.ds(late_at, q_loc), :]], axis=1)
+                to_modal(f, ypart[f] + dot(ltab[...], right_terms(x)))
+        else:
+            @pl.loop(0, half, unroll=UNROLL)
+            def _(f):
+                to_modal(f, products(f))
 
         first = pl.multiple_of(me * cell_dev + j * LANES, LANES)
         position = first + iota((1, LANES), 1)
-        weight = jnp.where(position < live, w_ref[:, pl.ds(first, LANES)] / total, 0.0)
+        weight = jnp.where(position < live, w_ref[pl.ds(me * subs + j, 1), :] / total, 0.0)
         block = iota((snaps, LANES), 1) // snaps
         steps = SUB // part
 
-        @pl.loop(0, modes // pack // steps)
-        def _(h):
+        def gram(h):
             rows = []
             for u in range(steps):
                 at = pl.multiple_of((h * steps + u) * LANES, LANES)
@@ -179,30 +218,12 @@
                 else:
                     acc[g, pl.ds(at, SUB), :] += new
 
-    def share(o):
-        other, device = peer(o)
-        return pltpu.make_async_remote_copy(
-            src_ref=acc.at[other], dst_ref=reda.at[grp],
-            send_sem=sa_sem.at[other], recv_sem=ra_sem.at[grp],
-            device_id=device, device_id_type=MESH)
-
-    def shared(o):
-        other, device = peer(o)
-        return pltpu.make_async_remote_copy(
-            src_ref=acc.at[other], dst_ref=reda.at[other],
-            send_sem=sa_sem.at[other], recv_sem=ra_sem.at[other],
-            device_id=device, device_id_type=MESH)
-
-    for o in range(1, n_grp):
-        share(o).start()
-    for o in range(1, n_grp):
-        shared(o).wait_recv()
-    rows = sb.shape[1]
-    for s in range(n_sec):
-        value = acc[grp, s * rows:(s + 1) * rows, :]
-        for o in range(1, n_grp):
-            value += reda[peer(o)[0], s * rows:(s + 1) * rows, :]
-        sb[s] = value
+        count = modes // pack // steps // STAGES
+        for t in range(STAGES):
+            pl.loop(t * count, (t + 1) * count, unroll=UNROLL)(gram)
+            if j == subs - 1:
+                for o in range(1, n_grp):
+                    share(o, t).start()
 
     def last(s, slot):
         return pltpu.make_async_remote_copy(
@@ -210,8 +231,20 @@
             send_sem=sb_sem.at[s], recv_sem=rb_sem.at[slot],
             device_id={"sec": s}, device_id_type=MESH)
 
-    for o in range(1, n_sec):
-        last(lax.rem(me + o, n_sec), me).start()
+    rows = sb.shape[1]
+    for t in range(STAGES):
+        for o in range(1, n_grp):
+            share(o, t, True).wait_recv()
+        for s in range(t * n_sec // STAGES, (t + 1) * n_sec // STAGES):
+            value = acc[grp, s * rows:(s + 1) * rows, :]
+            for o in range(1, n_grp):
+                value += reda[peer(o)[0], s * rows:(s + 1) * rows, :]
+            sb[s] = value
+
+            @pl.when(me != s)
+            def _():
+                last(s, me).start()
+
     value = sb[me]
     for o in range(1, n_sec):
         s = lax.rem(me + o, n_sec)
@@ -223,8 +256,9 @@
         @pl.loop(1, n_sec)
         def _(i):
             outgoing(i, j).wait_send()
-    for o in range(1, n_grp):
-        share(o).wait_send()
+    for t in range(STAGES):
+        for o in range(1, n_grp):
+            share(o, t).wait_send()
     for o in range(1, n_sec):
         last(lax.rem(me + o, n_sec), me).wait_send()
 
@@ -257,13 +291,15 @@
             pltpu.VMEM((n_sec, own_rows, LANES), F32),
             pltpu.VMEM((snaps * SUB, 3 * snaps * SUB), BF16),
             pltpu.VMEM((2 * modes, 3 * angles), BF16),
+            pltpu.VMEM((2 * modes, 3 * q_loc), BF16),
+            pltpu.VMEM((snaps // 2, 2 * modes, 2 * LANES), F32),
             dma((subs, n_sec)), dma((subs, n_sec)), dma((subs,)),
-            dma((n_grp,)), dma((n_grp,)), dma((n_sec,)), dma((n_sec,)),
+            dma((STAGES, n_grp)), dma((STAGES, n_grp)), dma((n_sec,)), dma((n_sec,)),
         ],
         compiler_params=pltpu.CompilerParams(
             collective_id=0, has_side_effects=True, vmem_limit_bytes=60 * 2**20),
         name="spod",
-    )(pressure, cell_weight.reshape(1, cells), live_cells, mode_order.reshape(1, modes))
+    )(pressure, cell_weight.reshape(cells // LANES, LANES), live_cells, mode_order.reshape(1, modes))
     out = packed.reshape(modes // pack // n_sec, part, pack, snaps)
     return out.transpose(0, 2, 1, 3).reshape(modes // n_sec, part, snaps)
 

time: 211 us -> 203 us (0.962)
  Pallas kernels: 209 us -> 201 us
    pallas_call x1, Pallas kernels: 209 us -> 201 us  [on_device(): pl.pallas_call(functools.partial(kernel, n_sec, n_tile, n_role), out_shap...]
where the time goes in v2:
time: 203 us
  Pallas kernels  201 us (99%)
    pallas_call x1, Pallas kernels, on_device(): pl.pallas_call(functools.partial(kernel, n_sec, n_tile, n_role), out_shap...  201 us

profile of v2, /device:TPU:0, one launch (start us, length us, event | category | flops | bytes accessed | tf_op | source)
XLA Modules:
  0.0 202.6 jit_solution(12844651476442524501)
XLA Ops:
  0.0 201.2 %spod.1 = f32[32,128]{1,0:T(8,128)} custom-call(f32[32,64,1024]{2,1,0:T(8,128)} %p_ref.1, f32[8,128]{1,0:T(8,128)} %bitcast.5, s32[8]{0:T(128)} %live_ref.1, s32[1,128]{1,0:T(1,128)} %bitcast.6), custom_call_target="tpu_custom_call" | custom-call | tf_op jit(solution)/shard_map/spod/pallas_call | solution.py:279
  201.2 0.8 reshape.14
  202.0 0.6 copy.5

commit v3 on v2

--- a/solution.py
+++ b/solution.py
@@ -37,8 +37,7 @@
     return lax.dot_general(a, b, dims, preferred_element_type=F32)
 
 
-def partner(i, me, n):
-    x = jnp.where(i == 1, n - 1, i - 1)
+def partner(x, me, n):
     other, bit = 0, 1
     while bit < n:
         other += (me // bit + x // bit) % 2 * bit
@@ -71,12 +70,14 @@
 
 
 def kernel(n_sec, n_tile, n_role, p_ref, w_ref, live_ref, mode_ref, out_ref,
-           recv, spec, zbuf, acc, reda, sb, redb, ttab, atab, ltab, ypart,
-           send_sem, recv_sem, own_sem, sa_sem, ra_sem, sb_sem, rb_sem):
+           recv, spec, zbuf, acc, pbuf, pacc, reda, sb, redb, ttab, atab, ltab, ypart,
+           send_sem, recv_sem, own_sem, pa_sem, pr_sem, sa_sem, ra_sem, sb_sem, rb_sem):
     me = lax.axis_index("sec")
     tile, role = lax.axis_index("tile"), lax.axis_index("role")
     n_grp = n_tile * n_role
     grp = tile * n_role + role
+    near = n_grp // 2
+    side, mine = tile % 2, tile // 2 * n_role + role
     snaps, q_loc, cells = p_ref.shape
     half = snaps // 2
     angles = q_loc * n_sec
@@ -141,14 +142,28 @@
 
     stage_rows = acc.shape[1] // STAGES
 
+    def pair(t):
+        at = pl.ds(t * stage_rows, stage_rows)
+        return pltpu.make_async_remote_copy(
+            src_ref=acc.at[pl.ds((1 - side) * near, near), at, :], dst_ref=pbuf.at[:, at, :],
+            send_sem=pa_sem.at[t], recv_sem=pr_sem.at[t],
+            device_id={"tile": tile + 1 - 2 * side}, device_id_type=MESH)
+
     def share(o, t, arriving=False):
-        other, device = peer(o)
+        other = lax.rem(mine + o, near)
         at = pl.ds(t * stage_rows, stage_rows)
-        slot = other if arriving else grp
+        slot = other if arriving else mine
         return pltpu.make_async_remote_copy(
-            src_ref=acc.at[other, at, :], dst_ref=reda.at[slot, at, :],
+            src_ref=pacc.at[other, at, :], dst_ref=reda.at[slot, at, :],
             send_sem=sa_sem.at[t, other], recv_sem=ra_sem.at[t, slot],
-            device_id=device, device_id_type=MESH)
+            device_id={"tile": other // n_role * 2 + side, "role": other % n_role}, device_id_type=MESH)
+
+    def forward(t):
+        pair(t).wait_recv()
+        at = pl.ds(t * stage_rows, stage_rows)
+        pacc[:, at, :] = acc[pl.ds(side * near, near), at, :] + pbuf[:, at, :]
+        for o in range(1, near):
+            share(o, t).start()
 
     def arrive(i, j):
         src = partner(i, me, n_sec)
@@ -213,17 +228,19 @@
             at = pl.multiple_of(h * SUB, SUB)
             for g in range(n_grp):
                 new = jnp.concatenate([r[g * part:(g + 1) * part] for r in rows], axis=0)
+                to = g // n_role % 2 * near + g // n_role // 2 * n_role + g % n_role
                 if j == 0:
-                    acc[g, pl.ds(at, SUB), :] = new
+                    acc[to, pl.ds(at, SUB), :] = new
                 else:
-                    acc[g, pl.ds(at, SUB), :] += new
+                    acc[to, pl.ds(at, SUB), :] += new
 
         count = modes // pack // steps // STAGES
         for t in range(STAGES):
             pl.loop(t * count, (t + 1) * count, unroll=UNROLL)(gram)
             if j == subs - 1:
-                for o in range(1, n_grp):
-                    share(o, t).start()
+                pair(t).start()
+                if t > 0:
+                    forward(t - 1)
 
     def last(s, slot):
         return pltpu.make_async_remote_copy(
@@ -231,14 +248,15 @@
             send_sem=sb_sem.at[s], recv_sem=rb_sem.at[slot],
             device_id={"sec": s}, device_id_type=MESH)
 
+    forward(STAGES - 1)
     rows = sb.shape[1]
     for t in range(STAGES):
-        for o in range(1, n_grp):
+        for o in range(1, near):
             share(o, t, True).wait_recv()
         for s in range(t * n_sec // STAGES, (t + 1) * n_sec // STAGES):
-            value = acc[grp, s * rows:(s + 1) * rows, :]
-            for o in range(1, n_grp):
-                value += reda[peer(o)[0], s * rows:(s + 1) * rows, :]
+            value = pacc[mine, s * rows:(s + 1) * rows, :]
+            for o in range(1, near):
+                value += reda[lax.rem(mine + o, near), s * rows:(s + 1) * rows, :]
             sb[s] = value
 
             @pl.when(me != s)
@@ -257,7 +275,8 @@
         def _(i):
             outgoing(i, j).wait_send()
     for t in range(STAGES):
-        for o in range(1, n_grp):
+        pair(t).wait_send()
+        for o in range(1, near):
             share(o, t).wait_send()
     for o in range(1, n_sec):
         last(lax.rem(me + o, n_sec), me).wait_send()
@@ -286,7 +305,9 @@
             pltpu.VMEM((snaps, angles, LANES), F32),
             pltpu.VMEM((modes * snaps, LANES), F32),
             pltpu.VMEM((n_grp, rows, LANES), F32),
-            pltpu.VMEM((n_grp, rows, LANES), F32),
+            pltpu.VMEM((n_grp // 2, rows, LANES), F32),
+            pltpu.VMEM((n_grp // 2, rows, LANES), F32),
+            pltpu.VMEM((n_grp // 2, rows, LANES), F32),
             pltpu.VMEM((n_sec, own_rows, LANES), F32),
             pltpu.VMEM((n_sec, own_rows, LANES), F32),
             pltpu.VMEM((snaps * SUB, 3 * snaps * SUB), BF16),
@@ -294,7 +315,7 @@
             pltpu.VMEM((2 * modes, 3 * q_loc), BF16),
             pltpu.VMEM((snaps // 2, 2 * modes, 2 * LANES), F32),
             dma((subs, n_sec)), dma((subs, n_sec)), dma((subs,)),
-            dma((STAGES, n_grp)), dma((STAGES, n_grp)), dma((n_sec,)), dma((n_sec,)),
+            dma((STAGES,)), dma((STAGES,)), dma((STAGES, n_grp // 2)), dma((STAGES, n_grp // 2)), dma((n_sec,)), dma((n_sec,)),
         ],
         compiler_params=pltpu.CompilerParams(
             collective_id=0, has_side_effects=True, vmem_limit_bytes=60 * 2**20),

time: 203 us -> 202 us (level)
  no operation moved by 1% of the time
where the time goes in v3:
time: 202 us
  Pallas kernels  200 us (99%)
    pallas_call x1, Pallas kernels, on_device(): pl.pallas_call(functools.partial(kernel, n_sec, n_tile, n_role), out_shap...  200 us

profile of v3, /device:TPU:0, one launch (start us, length us, event | category | flops | bytes accessed | tf_op | source)
XLA Modules:
  0.0 201.6 jit_solution(9962505560167518558)
XLA Ops:
  0.0 200.1 %spod.1 = f32[32,128]{1,0:T(8,128)} custom-call(f32[32,64,1024]{2,1,0:T(8,128)} %p_ref.1, f32[8,128]{1,0:T(8,128)} %bitcast.5, s32[8]{0:T(128)} %live_ref.1, s32[1,128]{1,0:T(1,128)} %bitcast.6), custom_call_target="tpu_custom_call" | custom-call | tf_op jit(solution)/shard_map/spod/pallas_call | solution.py:298
  200.1 0.8 reshape.14
  201.0 0.6 copy.5
